TPU v7x, 256 devices: a whole 4x4x8 slice. The times are simulated.
256 devices in a mesh: dp: 32 (over z, x_hi, core), row: 4 (over y), col: 2 (over x_lo).
Axes of the slice: x: 4 (x_hi: 2, x_lo: 2; x = x_hi * 2 + x_lo), y: 4, z: 8, core: 2. Of those that a mesh axis runs over, the one named last changes fastest.
Arguments:
- tokens: bfloat16 [6144, 4096], P('dp', ('row', 'col')), may hold values from -6 to 6
- in_weight: bfloat16 [4096, 3, 4096], P('dp', None, ('row', 'col')), may hold values from -0.09375 to 0.09375
- short_filter: float32 [3, 3, 4096], P(None, None, ('row', 'col')), may hold values from -3 to 3
- long_filter: bfloat16 [256, 128], P(('row', 'col')), may hold values from -0.59765625 to 0.59765625
- grad_out: bfloat16 [6144, 4096], P('dp', ('row', 'col')), may hold values from -6 to 6
Outputs:
- mixed: bfloat16 [6144, 4096], P('dp', ('row', 'col'))
- grad_in: bfloat16 [6144, 4096], P('dp', ('row', 'col'))
- grad_weight: float32 [4096, 3, 4096], P('dp', None, ('row', 'col'))
- grad_long: float32 [256, 128], P(('row', 'col'))
- grad_short: float32 [3, 3, 4096], P(None, None, ('row', 'col'))
All inputs are finite; a program needn't handle non-finite values.
Results may differ from a plain program's by a relative error of at most 0.019.
Values may be sent and summed in bfloat16 or wider, within the bound.
A program may use at most 128 MiB of HBM per device.

v0:
```python
import jax
import jax.numpy as jnp
from jax import lax
from jax.sharding import PartitionSpec as P


def from_behind(block, axis, distance):
    devices = range(lax.axis_size(axis))
    route = [(i - distance, i) for i in devices if i - distance in devices]
    return lax.ppermute(block, axis, route)


def toeplitz(leading, rows, span):
    groups = leading.shape[0]
    width = rows + span
    seed_row = jnp.concatenate(
        [leading, jnp.zeros((groups, width - leading.shape[1]), leading.dtype)], axis=1
    )
    tiled = jnp.tile(seed_row, (1, rows))
    skewed = tiled[:, : rows * (width - 1)].reshape(groups, rows, width - 1)
    return skewed[:, :, :span]


def to_groups(values, ngroups, members):
    count = values.shape[0]
    return values.reshape(count, ngroups, members).transpose(1, 2, 0)


def from_groups(values):
    groups, members, count = values.shape
    return values.transpose(2, 0, 1).reshape(count, groups * members)


def per_device(tokens, in_weight, short_filter, long_filter, grad_out):
    rows = tokens.shape[0]
    local = grad_out.shape[1]
    nshort = short_filter.shape[0]
    ntaps = long_filter.shape[1]
    ngroups = long_filter.shape[0]
    members = local // ngroups
    margin = ntaps - 1
    span = rows + margin
    scale = float(rows * lax.axis_size("dp")) ** (-0.5)
    whole = lax.all_gather(tokens, ("row", "col"), axis=1, tiled=True)
    full_w = lax.all_gather(in_weight, "dp", axis=0, tiled=True)
    mixed_in = jnp.einsum("sd,dic->sic", whole, full_w, preferred_element_type=jnp.float32).astype(
        jnp.bfloat16
    )
    before = from_behind(mixed_in[rows - margin - nshort + 1 :], "dp", 1)
    extended = jnp.concatenate([before, mixed_in], axis=0).astype(jnp.float32)
    long_feats = jnp.zeros((span, 3, local), jnp.float32)
    for j in range(nshort):
        long_feats = (
            long_feats + short_filter[j][None] * extended[nshort - 1 - j : nshort - 1 - j + span]
        )
    product_ext = (long_feats[:, 1] * long_feats[:, 2]).astype(jnp.bfloat16)
    feats = long_feats[margin:]
    short_rows = extended[margin:]
    product_cols = to_groups(product_ext, ngroups, members)
    causal = toeplitz(long_filter[:, ::-1], rows, span)
    conv = from_groups(
        jnp.einsum("gst,gct->gcs", causal, product_cols, preferred_element_type=jnp.float32)
    )
    mixed = (feats[:, 0] * conv).astype(jnp.bfloat16)
    upstream = grad_out.astype(jnp.float32)
    grad_query = upstream * conv
    grad_conv = (upstream * feats[:, 0]).astype(jnp.bfloat16)
    after = from_behind(grad_conv[:margin], "dp", -1)
    grad_ext = jnp.concatenate([grad_conv, after], axis=0)
    anti = toeplitz(long_filter, rows, span)
    grad_product = from_groups(
        jnp.einsum(
            "gst,gct->gcs",
            anti,
            to_groups(grad_ext, ngroups, members),
            preferred_element_type=jnp.float32,
        )
    )
    reversed_cols = jnp.concatenate(
        [product_cols[:, :, ::-1], jnp.zeros((ngroups, members, rows), product_cols.dtype)], axis=2
    )
    width = span + rows
    pairs = jnp.einsum(
        "gcs,gcu->gsu",
        to_groups(grad_conv, ngroups, members),
        reversed_cols,
        preferred_element_type=jnp.float32,
    )
    diagonal = pairs.reshape(ngroups, rows * width)[:, : rows * (width - 1)].reshape(
        ngroups, rows, width - 1
    )
    filter_part = jnp.sum(diagonal[:, :, rows - 1 : rows - 1 + ntaps], axis=1)
    grad_feats = jnp.stack(
        [grad_query, grad_product * feats[:, 2], grad_product * feats[:, 1]], axis=1
    )
    later = from_behind(grad_feats[: nshort - 1], "dp", -1)
    feats_ext = jnp.concatenate([grad_feats, later], axis=0)
    grad_acc = jnp.zeros((rows, 3, local), jnp.float32)
    for j in range(nshort):
        grad_acc = grad_acc + short_filter[j][None] * feats_ext[j : j + rows]
    grad_mixed = grad_acc.astype(jnp.bfloat16)
    short_part = jnp.stack(
        [
            jnp.sum(grad_feats * short_rows[nshort - 1 - j : nshort - 1 - j + rows], axis=0)
            for j in range(nshort)
        ]
    )
    filter_total, short_total = (
        lax.psum(filter_part.astype(jnp.bfloat16), "dp").astype(jnp.float32),
        lax.psum(short_part.astype(jnp.bfloat16), "dp").astype(jnp.float32),
    )
    grad_long = filter_total * scale
    grad_short = short_total * scale
    partial_in = jnp.einsum("sic,dic->sd", grad_mixed, full_w, preferred_element_type=jnp.float32)
    summed_in = lax.psum_scatter(
        partial_in.astype(jnp.bfloat16), ("row", "col"), scatter_dimension=1, tiled=True
    )
    weight_term = (
        jnp.einsum("sd,sic->dic", whole, grad_mixed, preferred_element_type=jnp.float32) * scale
    )
    grad_weight = lax.psum_scatter(
        weight_term.astype(jnp.bfloat16), "dp", scatter_dimension=0, tiled=True
    ).astype(jnp.float32)
    return (mixed, summed_in, grad_weight, grad_long, grad_short)


def solution(mesh):
    placed = (
        P("dp", ("row", "col")),
        P("dp", None, ("row", "col")),
        P(None, None, ("row", "col")),
        P(("row", "col"), None),
        P("dp", ("row", "col")),
    )
    return jax.shard_map(
        per_device,
        mesh=mesh,
        in_specs=placed,
        out_specs=(
            P("dp", ("row", "col")),
            P("dp", ("row", "col")),
            P("dp", None, ("row", "col")),
            P(("row", "col"), None),
            P(None, None, ("row", "col")),
        ),
        check_vma=False,
    )
```

profile of v0, /device:TPU:4, one launch (start us, length us, event | category | flops | bytes accessed | tf_op | source)
XLA Modules:
  0.0 539.4 jit_solution(406576866576352220)
XLA Ops:
  8.7 48.7 %all-gather.3.cloned.1.call-done = bf16[192,4096]{1,0:T(8,128)(2,1)} async-done(((bf16[192,512]{1,0:T(8,128)(2,1)}), bf16[192,4096]{1,0:T(8,128)(2,1)}) %all-gather.3.cloned.1.call-update) | async-done | bytes 1572880 | tf_op jit(solution)/shard_map/all_gather | solution.py:44
  57.4 117.2 %all-gather.5.cloned.1.call-done = bf16[4096,3,512]{2,0,1:T(8,128)(2,1)} async-done(((bf16[128,3,512]{2,0,1:T(8,128)(2,1)}), bf16[4096,3,512]{2,0,1:T(8,128)(2,1)}) %all-gather.5.cloned.1.call-update) | async-done | bytes 12582928 | tf_op jit(solution)/shard_map/all_gather | solution.py:45
  174.6 7.7 %fusion.10 = bf16[192,3,512]{2,0,1:T(8,128)(2,1)S(1)} fusion(bf16[4096,3,512]{2,0,1:T(8,128)(2,1)} %all-gather.5.cloned.1.call-done, bf16[192,4096]{1,0:T(8,128)(2,1)} %all-gather.3.cloned.1.call-done), kind=kOutput, calls=%fused_computation.16 | convolution fusion | flops 2416214016 | bytes 14745600 | tf_op jit(solution)/shard_map/sd,dic->sic/dot_general | solution.py:46
  184.7 3.1 tile.8
  187.8 11.6 %tile.9 = bf16[32,98112]{1,0:T(8,128)(2,1)} reshape(bf16[32,192,511]{2,1,0:T(8,128)(2,1)} %tile.8) | data formatting | bytes 12558336 | tf_op jit(solution)/shard_map/tile | solution.py:19
  199.4 5.8 %slice.119 = bf16[32,97920]{1,0:T(8,128)(2,1)} slice(bf16[32,98112]{1,0:T(8,128)(2,1)} %tile.9), slice={[0:32], [0:97920]} | slice | bytes 12533760 | tf_op jit(solution)/shard_map/slice | solution.py:20
  205.3 15.3 %reshape.49 = bf16[32,192,510]{2,1,0:T(8,128)(2,1)} reshape(bf16[32,97920]{1,0:T(8,128)(2,1)} %slice.119) | data formatting | bytes 12533760 | tf_op jit(solution)/shard_map/reshape | solution.py:20
  223.1 4.1 fusion.3
  230.0 5.1 collective-permute-start.1
  235.2 3.2 tile.20
  238.3 11.6 %tile.21 = bf16[32,98112]{1,0:T(8,128)(2,1)} reshape(bf16[32,192,511]{2,1,0:T(8,128)(2,1)} %tile.20) | data formatting | bytes 12558336 | tf_op jit(solution)/shard_map/tile | solution.py:19
  249.9 5.8 %slice.122 = bf16[32,97920]{1,0:T(8,128)(2,1)} slice(bf16[32,98112]{1,0:T(8,128)(2,1)} %tile.21), slice={[0:32], [0:97920]} | slice | bytes 12533760 | tf_op jit(solution)/shard_map/slice | solution.py:20
  255.8 15.3 %reshape.52 = bf16[32,192,510]{2,1,0:T(8,128)(2,1)} reshape(bf16[32,97920]{1,0:T(8,128)(2,1)} %slice.122) | data formatting | bytes 12533760 | tf_op jit(solution)/shard_map/reshape | solution.py:20
  272.0 4.2 fusion.1
  283.6 6.6 %multiply_convert_fusion = bf16[3,512,4096]{2,1,0:T(8,128)(2,1)} fusion(bf16[192,3,512]{2,0,1:T(8,128)(2,1)S(1)} %get-tuple-element.29, bf16[192,4096]{1,0:T(8,128)(2,1)S(1)} %copy-done.6), kind=kOutput, calls=%fused_computation | convolution fusion | flops 2428502016 | bytes 14745600 | tf_op jit(solution)/shard_map/sd,sic->dic/dot_general | solution.py:119
  290.2 16.6 %copy.34 = bf16[4096,1536]{1,0:T(8,128)(2,1)} copy(bf16[4096,1536]{0,1:T(8,128)(2,1)} %bitcast.62) | data formatting | bytes 25165824
  307.9 10.0 %fusion = bf16[192,4096]{1,0:T(8,128)(2,1)} fusion(bf16[192,3,512]{2,0,1:T(8,128)(2,1)S(1)} %copy-done.2, bf16[4096,3,512]{2,0,1:T(8,128)(2,1)} %all-gather.5.cloned.1.call-done), kind=kOutput, calls=%fused_computation.2 | convolution fusion | flops 2416705536 | bytes 14745600 | tf_op jit(solution)/shard_map/sic,dic->sd/dot_general | solution.py:114
  318.8 6.9 %fusion.20 = f32[32,192,511]{2,1,0:T(8,128)} fusion(bf16[32,16,192]{2,1,0:T(8,128)(2,1)S(1)} %bitcast.69, bf16[32,16,319]{2,1,0:T(8,128)(2,1)S(1)} %slice.183), kind=kOutput, calls=%fused_computation.33 | convolution fusion | flops 100466688 | bytes 13081600 | tf_op jit(solution)/shard_map/gcs,gcu->gsu/dot_general | solution.py:83
  325.7 13.2 %reshape.55 = f32[32,98112]{1,0:T(8,128)} reshape(f32[32,192,511]{2,1,0:T(8,128)} %fusion.20) | data formatting | bytes 25116672 | tf_op jit(solution)/shard_map/reshape | solution.py:89
  338.8 11.4 %slice.129 = f32[32,97920]{1,0:T(8,128)} slice(f32[32,98112]{1,0:T(8,128)} %reshape.55), slice={[0:32], [0:97920]} | slice | bytes 25067520 | tf_op jit(solution)/shard_map/slice | solution.py:89
  350.3 15.2 %reshape.56 = f32[32,192,510]{2,1,0:T(8,128)} reshape(f32[32,97920]{1,0:T(8,128)} %slice.129) | data formatting | bytes 25067520 | tf_op jit(solution)/shard_map/reshape | solution.py:89
  365.5 4.4 slice_reduce_fusion
  369.9 127.2 %all-reduce.3 = (bf16[32,128]{1,0:T(8,128)(2,1)S(1)}, bf16[3,3,512]{2,1,0:T(4,128)(2,1)S(1)}) all-reduce(bf16[32,128]{1,0:T(8,128)(2,1)S(1)} %slice_reduce_fusion, bf16[3,3,512]{2,1,0:T(4,128)(2,1)S(1)} %pad_maximum_fusion.3), channel_id=1, replica_groups=mesh['dp'=32,'row'=4,'col'=2] {'dp'}, use_global_device_ids=true, to_apply=%region_3.0 | all-reduce | flops 8704 | bytes 34816 | tf_op jit(solution)/shard_map/psum | solution.py:109
  500.7 32.2 %reduce-scatter.5.cloned.1.call-done = bf16[192,512]{1,0:T(8,128)(2,1)} async-done(((bf16[192,4096]{1,0:T(8,128)(2,1)}), bf16[192,512]{1,0:T(8,128)(2,1)}) %reduce-scatter.5.cloned.1.call-update) | async-done | bytes 196624 | tf_op jit(solution)/shard_map/reduce_scatter | solution.py:115
  (56 shorter events, 22.8 us)
Async XLA Ops:
  7.2 50.3 %all-gather.3.cloned.1.call-start = ((), (), s32[]{:S(2)}) async-start(), calls=%async_computation.2 | async-start | bytes 1769472 | tf_op jit(solution)/shard_map/all_gather | solution.py:44
  7.9 166.7 %all-gather.5.cloned.1.call-start = ((), (), s32[]{:S(2)}) async-start(), calls=%async_computation.3 | async-start | bytes 12976128 | tf_op jit(solution)/shard_map/all_gather | solution.py:45
  8.6 175.9 %copy-start.4 = (bf16[32,128]{1,0:T(8,128)(2,1)S(1)}, bf16[32,128]{1,0:T(8,128)(2,1)}, u32[]{:S(2)}) copy-start(bf16[32,128]{1,0:T(8,128)(2,1)} %param.8) | copy-start | bytes 24580
  8.7 489.7 %reduce-scatter.7.cloned.1.call-start = ((), (), s32[]{:S(2)}) async-start(), calls=%async_computation.5 | async-start | bytes 12976128
  182.4 38.2 %collective-permute-start = (bf16[129,3,512]{2,0,1:T(8,128)(2,1)S(1)}, bf16[129,3,512]{2,0,1:T(8,128)(2,1)S(1)}, u32[]{:S(2)}, u32[]{:S(2)}) collective-permute-start(bf16[129,3,512]{2,0,1:T(8,128)(2,1)S(1)} %slice.112), channel_id=1, source_target_pairs={{0,8},{8,16},{16,24},{24,32},{32,40},{40,48},{48,56},{56,64},{64,7... | collective-permute-start | bytes 1188872 | tf_op jit(solution)/shard_map/ppermute | solution.py:10
  205.3 15.3 %copy-start.5 = (f32[3,3,512]{2,1,0:T(4,128)S(1)}, f32[3,3,512]{2,1,0:T(4,128)}, u32[]{:S(2)}) copy-start(f32[3,3,512]{2,1,0:T(4,128)} %param.7) | copy-start | bytes 55300
  221.5 1.3 copy-start
  223.1 5.1 copy-start.3
  230.0 41.0 %collective-permute-start.1 = (bf16[127,512]{1,0:T(8,128)(2,1)S(1)}, bf16[127,512]{1,0:T(8,128)(2,1)S(1)}, u32[]{:S(2)}, u32[]{:S(2)}) collective-permute-start(bf16[127,512]{1,0:T(8,128)(2,1)S(1)} %slice.121), channel_id=1, source_target_pairs={{8,0},{16,8},{24,16},{32,24},{40,32},{48,40},{56,48},{64,56},{72,6... | collective-permute-start | bytes 390152 | tf_op jit(solution)/shard_map/ppermute | solution.py:10
  278.7 3.4 collective-permute-start.2
  282.2 1.4 copy-start.6
  283.0 7.2 %copy-start.1 = (bf16[192,3,512]{2,0,1:T(8,128)(2,1)}, bf16[192,3,512]{2,0,1:T(8,128)(2,1)S(1)}, u32[]{:S(2)}) copy-start(bf16[192,3,512]{2,0,1:T(8,128)(2,1)S(1)} %get-tuple-element.29) | copy-start | bytes 1769476
  306.8 1.1 copy-start.2
  306.9 226.0 %reduce-scatter.5.cloned.1.call-start = ((), (), s32[]{:S(2)}) async-start(), calls=%async_computation.4 | async-start | bytes 1769472 | tf_op jit(solution)/shard_map/reduce_scatter | solution.py:115
Sparse Core Ops, SparseCore 0:
  9.8 47.6 all-gather.2
  60.2 114.3 all-gather.4
  307.0 175.7 reduce-scatter.6
  485.8 47.0 reduce-scatter.4
where the time goes:
time: 540 us; the launch traced here: 539 us
  waiting for transfers between devices  201 us (37%)
  local copies, waits for them, and re-layouts  137 us (25%)
  blocking collectives  127 us (24%)
  matrix products  39.5 us (7%)
  between operations  14 us (3%)
  other arithmetic  10.9 us (2%)
  starting transfers between devices  9.64 us (2%)
    psum x1, blocking collectives, per_device(): lax.psum(filter_part.astype(jnp.bfloat16), 'dp').astype(jnp.float32)  127 us
    all_gather x1, waiting for transfers between devices, per_device(): full_w = lax.all_gather(in_weight, 'dp', axis=0, tiled=True)  117 us
    all_gather x1, waiting for transfers between devices, per_device(): whole = lax.all_gather(tokens, ('row', 'col'), axis=1, tiled=True)  48.7 us
    reduce_scatter x1, waiting for transfers between devices, per_device(): lax.psum_scatter(partial_in.astype(jnp.bfloat16), ('row', 'col'), scatter...  32.2 us
    reshape x2, local copies, waits for them, and re-layouts, toeplitz(): skewed = tiled[:, :rows * (width - 1)].reshape(groups, rows, width - 1)  30.6 us
    another operation x4, local copies, waits for them, and re-layouts, toeplitz(): tiled = jnp.tile(seed_row, (1, rows))  29.5 us
    reshape x2, local copies, waits for them, and re-layouts, per_device(): pairs.reshape(ngroups, rows * width)[:, :rows * (width - 1)]  28.4 us
    unnamed x19, local copies, waits for them, and re-layouts  22.2 us
  transfers between devices with their start and end apart: 7, of which 4 were waited for; matrix products, arithmetic and copies ran while one was open for 25% of the time, Pallas kernels for 0%

commit v1 on v0

--- a/solution.py
+++ b/solution.py
@@ -41,7 +41,7 @@
     margin = ntaps - 1
     span = rows + margin
     scale = float(rows * lax.axis_size("dp")) ** (-0.5)
-    whole = lax.all_gather(tokens, ("row", "col"), axis=1, tiled=True)
+    whole = jnp.concatenate(lax.all_gather(tokens, ("row", "col")), axis=1)
     full_w = lax.all_gather(in_weight, "dp", axis=0, tiled=True)
     mixed_in = jnp.einsum("sd,dic->sic", whole, full_w, preferred_element_type=jnp.float32).astype(
         jnp.bfloat16

time: 540 us -> 541 us (level)
  transfers between devices with their start and end apart: 7 -> 7, of which waited for: 4 -> 4; matrix products, arithmetic and copies ran while one was open for 25% -> 26% of each run, Pallas kernels for 0% -> 0%
where the time goes in v1:
time: 541 us; the launch traced here: 539 us
  waiting for transfers between devices  196 us (36%)
  local copies, waits for them, and re-layouts  142 us (26%)
  blocking collectives  127 us (23%)
  matrix products  39.5 us (7%)
  between operations  14 us (3%)
  other arithmetic  10.9 us (2%)
  starting transfers between devices  9.64 us (2%)
    psum x1, blocking collectives, per_device(): lax.psum(filter_part.astype(jnp.bfloat16), 'dp').astype(jnp.float32)  127 us
    all_gather x1, waiting for transfers between devices, per_device(): full_w = lax.all_gather(in_weight, 'dp', axis=0, tiled=True)  113 us
    all_gather x1, waiting for transfers between devices, per_device(): whole = jnp.concatenate(lax.all_gather(tokens, ('row', 'col')), axis=1)  48.7 us
    reduce_scatter x1, waiting for transfers between devices, per_device(): lax.psum_scatter(partial_in.astype(jnp.bfloat16), ('row', 'col'), scatter...  32.1 us
    reshape x2, local copies, waits for them, and re-layouts, toeplitz(): skewed = tiled[:, :rows * (width - 1)].reshape(groups, rows, width - 1)  30.6 us
    another operation x4, local copies, waits for them, and re-layouts, toeplitz(): tiled = jnp.tile(seed_row, (1, rows))  29.5 us
    reshape x2, local copies, waits for them, and re-layouts, per_device(): pairs.reshape(ngroups, rows * width)[:, :rows * (width - 1)]  28.4 us
    unnamed x19, local copies, waits for them, and re-layouts  22.2 us
  transfers between devices with their start and end apart: 7, of which 4 were waited for; matrix products, arithmetic and copies ran while one was open for 26% of the time, Pallas kernels for 0%

profile of v1, /device:TPU:4, one launch (start us, length us, event | category | flops | bytes accessed | tf_op | source)
XLA Modules:
  0.0 539.4 jit_solution(2320550489860452767)
XLA Ops:
  8.7 48.7 %all-gather.6.cloned.1.call-done = bf16[1536,512]{1,0:T(8,128)(2,1)} async-done(((bf16[192,512]{1,0:T(8,128)(2,1)}), bf16[1536,512]{1,0:T(8,128)(2,1)}) %all-gather.6.cloned.1.call-update) | async-done | bytes 1572880 | tf_op jit(solution)/shard_map/all_gather | solution.py:44
  61.8 112.8 %all-gather.4.cloned.1.call-done = bf16[4096,3,512]{2,0,1:T(8,128)(2,1)} async-done(((bf16[128,3,512]{2,0,1:T(8,128)(2,1)}), bf16[4096,3,512]{2,0,1:T(8,128)(2,1)}) %all-gather.4.cloned.1.call-update) | async-done | bytes 12582928 | tf_op jit(solution)/shard_map/all_gather | solution.py:45
  174.6 7.7 %convolution_convert_fusion = bf16[192,3,512]{2,0,1:T(8,128)(2,1)S(1)} fusion(bf16[192,4096,1]{1,0,2:T(8,128)(2,1)} %reshape.66, bf16[4096,3,512]{2,0,1:T(8,128)(2,1)} %all-gather.4.cloned.1.call-done), kind=kOutput, calls=%fused_computation.14 | convolution fusion | flops 2416214016 | bytes 14745600 | tf_op jit(solution)/shard_map/sd,dic->sic/dot_general | solution.py:46
  184.7 3.1 tile.8
  187.8 11.6 %tile.9 = bf16[32,98112]{1,0:T(8,128)(2,1)} reshape(bf16[32,192,511]{2,1,0:T(8,128)(2,1)} %tile.8) | data formatting | bytes 12558336 | tf_op jit(solution)/shard_map/tile | solution.py:19
  199.4 5.8 %slice.119 = bf16[32,97920]{1,0:T(8,128)(2,1)} slice(bf16[32,98112]{1,0:T(8,128)(2,1)} %tile.9), slice={[0:32], [0:97920]} | slice | bytes 12533760 | tf_op jit(solution)/shard_map/slice | solution.py:20
  205.2 15.3 %reshape.57 = bf16[32,192,510]{2,1,0:T(8,128)(2,1)} reshape(bf16[32,97920]{1,0:T(8,128)(2,1)} %slice.119) | data formatting | bytes 12533760 | tf_op jit(solution)/shard_map/reshape | solution.py:20
  223.1 4.1 fusion.3
  230.0 5.1 collective-permute-start.1
  235.2 3.2 tile.20
  238.3 11.6 %tile.21 = bf16[32,98112]{1,0:T(8,128)(2,1)} reshape(bf16[32,192,511]{2,1,0:T(8,128)(2,1)} %tile.20) | data formatting | bytes 12558336 | tf_op jit(solution)/shard_map/tile | solution.py:19
  249.9 5.8 %slice.122 = bf16[32,97920]{1,0:T(8,128)(2,1)} slice(bf16[32,98112]{1,0:T(8,128)(2,1)} %tile.21), slice={[0:32], [0:97920]} | slice | bytes 12533760 | tf_op jit(solution)/shard_map/slice | solution.py:20
  255.8 15.3 %reshape.60 = bf16[32,192,510]{2,1,0:T(8,128)(2,1)} reshape(bf16[32,97920]{1,0:T(8,128)(2,1)} %slice.122) | data formatting | bytes 12533760 | tf_op jit(solution)/shard_map/reshape | solution.py:20
  272.0 4.2 fusion.1
  283.6 6.6 %multiply_convert_fusion = bf16[3,512,4096]{2,1,0:T(8,128)(2,1)} fusion(bf16[192,3,512]{2,0,1:T(8,128)(2,1)S(1)} %get-tuple-element.29, bf16[192,4096,1]{1,0,2:T(8,128)(2,1)S(1)} %copy-done.1), kind=kOutput, calls=%fused_computation | convolution fusion | flops 2428502016 | bytes 14745600 | tf_op jit(solution)/shard_map/sd,sic->dic/dot_general | solution.py:119
  290.2 16.6 %copy.37 = bf16[4096,1536]{1,0:T(8,128)(2,1)} copy(bf16[4096,1536]{0,1:T(8,128)(2,1)} %bitcast.61) | data formatting | bytes 25165824
  307.9 10.0 %fusion = bf16[192,4096]{1,0:T(8,128)(2,1)} fusion(bf16[192,3,512]{2,0,1:T(8,128)(2,1)S(1)} %copy-done.3, bf16[4096,3,512]{2,0,1:T(8,128)(2,1)} %all-gather.4.cloned.1.call-done), kind=kOutput, calls=%fused_computation.2 | convolution fusion | flops 2416705536 | bytes 14745600 | tf_op jit(solution)/shard_map/sic,dic->sd/dot_general | solution.py:114
  318.8 6.9 %fusion.14 = f32[32,192,511]{2,1,0:T(8,128)} fusion(bf16[32,16,192]{2,1,0:T(8,128)(2,1)S(1)} %bitcast.70, bf16[32,16,319]{2,1,0:T(8,128)(2,1)S(1)} %slice.183), kind=kOutput, calls=%fused_computation.31 | convolution fusion | flops 100466688 | bytes 13081600 | tf_op jit(solution)/shard_map/gcs,gcu->gsu/dot_general | solution.py:83
  325.7 13.2 %reshape.63 = f32[32,98112]{1,0:T(8,128)} reshape(f32[32,192,511]{2,1,0:T(8,128)} %fusion.14) | data formatting | bytes 25116672 | tf_op jit(solution)/shard_map/reshape | solution.py:89
  338.8 11.4 %slice.129 = f32[32,97920]{1,0:T(8,128)} slice(f32[32,98112]{1,0:T(8,128)} %reshape.63), slice={[0:32], [0:97920]} | slice | bytes 25067520 | tf_op jit(solution)/shard_map/slice | solution.py:89
  350.3 15.2 %reshape.64 = f32[32,192,510]{2,1,0:T(8,128)} reshape(f32[32,97920]{1,0:T(8,128)} %slice.129) | data formatting | bytes 25067520 | tf_op jit(solution)/shard_map/reshape | solution.py:89
  365.5 4.4 slice_reduce_fusion
  369.9 127.3 %all-reduce.3 = (bf16[32,128]{1,0:T(8,128)(2,1)S(1)}, bf16[3,3,512]{2,1,0:T(4,128)(2,1)S(1)}) all-reduce(bf16[32,128]{1,0:T(8,128)(2,1)S(1)} %slice_reduce_fusion, bf16[3,3,512]{2,1,0:T(4,128)(2,1)S(1)} %pad_maximum_fusion.3), channel_id=1, replica_groups=mesh['dp'=32,'row'=4,'col'=2] {'dp'}, use_global_device_ids=true, to_apply=%region_3.0 | all-reduce | flops 8704 | bytes 34816 | tf_op jit(solution)/shard_map/psum | solution.py:109
  500.8 32.1 %reduce-scatter.5.cloned.1.call-done = bf16[192,512]{1,0:T(8,128)(2,1)} async-done(((bf16[192,4096]{1,0:T(8,128)(2,1)}), bf16[192,512]{1,0:T(8,128)(2,1)}) %reduce-scatter.5.cloned.1.call-update) | async-done | bytes 196624 | tf_op jit(solution)/shard_map/reduce_scatter | solution.py:115
  (58 shorter events, 27.2 us)
Async XLA Ops:
  7.2 50.3 %all-gather.6.cloned.1.call-start = ((), (), s32[]{:S(2)}) async-start(), calls=%async_computation.4 | async-start | bytes 1769472 | tf_op jit(solution)/shard_map/all_gather | solution.py:44
  7.9 166.7 %all-gather.4.cloned.1.call-start = ((), (), s32[]{:S(2)}) async-start(), calls=%async_computation.2 | async-start | bytes 12976128 | tf_op jit(solution)/shard_map/all_gather | solution.py:45
  8.6 489.8 %reduce-scatter.7.cloned.1.call-start = ((), (), s32[]{:S(2)}) async-start(), calls=%async_computation.5 | async-start | bytes 12976128
  61.8 122.7 %copy-start.5 = (bf16[32,128]{1,0:T(8,128)(2,1)S(1)}, bf16[32,128]{1,0:T(8,128)(2,1)}, u32[]{:S(2)}) copy-start(bf16[32,128]{1,0:T(8,128)(2,1)} %param.8) | copy-start | bytes 24580
  182.4 38.2 %collective-permute-start = (bf16[129,3,512]{2,0,1:T(8,128)(2,1)S(1)}, bf16[129,3,512]{2,0,1:T(8,128)(2,1)S(1)}, u32[]{:S(2)}, u32[]{:S(2)}) collective-permute-start(bf16[129,3,512]{2,0,1:T(8,128)(2,1)S(1)} %slice.112), channel_id=1, source_target_pairs={{0,8},{8,16},{16,24},{24,32},{32,40},{40,48},{48,56},{56,64},{64,7... | collective-permute-start | bytes 1188872 | tf_op jit(solution)/shard_map/ppermute | solution.py:10
  205.2 15.3 %copy-start.6 = (f32[3,3,512]{2,1,0:T(4,128)S(1)}, f32[3,3,512]{2,1,0:T(4,128)}, u32[]{:S(2)}) copy-start(f32[3,3,512]{2,1,0:T(4,128)} %param.7) | copy-start | bytes 55300
  221.4 1.3 copy-start
  223.1 5.1 copy-start.4
  230.0 41.0 %collective-permute-start.1 = (bf16[127,512]{1,0:T(8,128)(2,1)S(1)}, bf16[127,512]{1,0:T(8,128)(2,1)S(1)}, u32[]{:S(2)}, u32[]{:S(2)}) collective-permute-start(bf16[127,512]{1,0:T(8,128)(2,1)S(1)} %slice.121), channel_id=1, source_target_pairs={{8,0},{16,8},{24,16},{32,24},{40,32},{48,40},{56,48},{64,56},{72,6... | collective-permute-start | bytes 390152 | tf_op jit(solution)/shard_map/ppermute | solution.py:10
  278.7 3.4 collective-permute-start.2
  282.2 1.4 copy-start.1
  283.0 7.2 %copy-start.2 = (bf16[192,3,512]{2,0,1:T(8,128)(2,1)}, bf16[192,3,512]{2,0,1:T(8,128)(2,1)S(1)}, u32[]{:S(2)}) copy-start(bf16[192,3,512]{2,0,1:T(8,128)(2,1)S(1)} %get-tuple-element.29) | copy-start | bytes 1769476
  306.9 1.1 copy-start.3
  306.9 226.0 %reduce-scatter.5.cloned.1.call-start = ((), (), s32[]{:S(2)}) async-start(), calls=%async_computation.3 | async-start | bytes 1769472 | tf_op jit(solution)/shard_map/reduce_scatter | solution.py:115
Sparse Core Ops, SparseCore 0:
  9.8 47.6 all-gather.5
  60.2 114.3 all-gather.3
  307.0 175.6 reduce-scatter.6
  485.7 47.1 reduce-scatter.4
